TPU v7x, 32 devices: a whole 2x2x4 slice. The times are simulated.
32 devices in a mesh: dp: 8 (over z, y), expert: 4 (over x, core).
Axes of the slice: x: 2, y: 2, z: 4, core: 2. Of those that a mesh axis runs over, the one named last changes fastest.
Arguments:
- tokens: bfloat16 [12288, 768], P(('dp', 'expert')), may hold values from -6 to 6
- groups: int32 [32, 384], P(('dp', 'expert')), may hold values from 0 to 1, never falling along the last dimension, each value on 1 to 261 neighbouring positions
- key_mask: int32 [12288], P(('dp', 'expert')), may hold values 0 or 1
- routes: int32 [12288, 1], P(('dp', 'expert')), may hold values from 0 to 2; in each aligned block of 384 rows (0 to 383, 384 to 767, ...) at most 144 rows name the same one
- query_weight: bfloat16 [2, 768, 768], P(None, ('dp', 'expert')), may hold values from -0.21875 to 0.21875
- key_weight: bfloat16 [2, 768, 768], P(None, ('dp', 'expert')), may hold values from -0.21875 to 0.21875
- value_weight: bfloat16 [2, 768, 768], P(None, ('dp', 'expert')), may hold values from -0.21875 to 0.21875
- output_weight: bfloat16 [2, 768, 768], P(None, ('dp', 'expert')), may hold values from -1.75 to 1.75
- norm_first: bfloat16 [2, 768], P(None, ('dp', 'expert')), may hold values from 0.25 to 1.75
- norm_second: bfloat16 [2, 768], P(None, ('dp', 'expert')), may hold values from 0.25 to 1.75
- expert_in: bfloat16 [2, 3, 768, 3072], P(None, None, 'dp', 'expert'), may hold values from -0.21875 to 0.21875
- expert_out: bfloat16 [2, 3, 3072, 768], P(None, None, 'expert', 'dp'), may hold values from -0.109375 to 0.109375
- cotangent: float32 [12288, 768], P(('dp', 'expert')), may hold values from -6 to 6
Outputs:
- mixed: bfloat16 [12288, 768], P(('dp', 'expert'))
- delta_tokens: float32 [12288, 768], P(('dp', 'expert'))
- delta_query: float32 [2, 768, 768], P(None, ('dp', 'expert'))
- delta_key: float32 [2, 768, 768], P(None, ('dp', 'expert'))
- delta_value: float32 [2, 768, 768], P(None, ('dp', 'expert'))
- delta_output: float32 [2, 768, 768], P(None, ('dp', 'expert'))
- delta_first: float32 [2, 768], P(None, ('dp', 'expert'))
- delta_second: float32 [2, 768], P(None, ('dp', 'expert'))
- delta_in: float32 [2, 3, 768, 3072], P(None, None, 'dp', 'expert')
- delta_out: float32 [2, 3, 3072, 768], P(None, None, 'expert', 'dp')
Inputs may be any that keep to these rules, and one draw needn't show every extreme that they name: Each device's block holds 2 groups numbered in order, each of 1 to 261 tokens. `routes`: among the 384 tokens of one device no expert is named more than 144 times; on some devices one expert is named exactly 144 times.
All inputs are finite; a program needn't handle non-finite values. No bound on the sum of `key_mask` on one device may be relied on, other than what follows from the above.
Results may differ from a plain program's by a relative error of at most 0.024.
Values may be sent and summed in bfloat16 or wider, within the bound.
No kernel may reach another device: no remote copies, remote signals or barrier semaphores. Data moves between devices by JAX's collectives and lax.ppermute only.
A program may use at most 256 MiB of HBM per device.

v0:
```python
from functools import partial
import jax
import jax.numpy as jnp
from jax import lax
from jax.sharding import PartitionSpec as P

HEADS = 12
HEAD_DIM = 64
EXPERTS = 3
LAYERS = 2
MOST = 144
epsilon = 1e-05
score_scale = 0.125


def layer_norm(values, gain_vector):
    average = jnp.mean(values, -1, keepdims=True)
    centered = values - average
    spread = jnp.mean(centered * centered, -1, keepdims=True)
    return centered * lax.rsqrt(spread + epsilon) * gain_vector


def contract_rows(left, right):
    return lax.dot_general(
        left, right, (((0,), (0,)), ((), ())), preferred_element_type=jnp.float32
    )


def contract_cols(left, right):
    return lax.dot_general(
        left, right, (((1,), (1,)), ((), ())), preferred_element_type=jnp.float32
    )


def slot_tables(route_row):
    row_count = route_row.shape[0]
    one_hot = (route_row[:, None] == jnp.arange(EXPERTS, dtype=jnp.int32)[None, :]).astype(
        jnp.int32
    )
    running = jnp.cumsum(one_hot, 0) - 1
    position = jnp.sum(running * one_hot, 1)
    slot_of = route_row * MOST + position
    token_of = (
        jnp.zeros((EXPERTS * MOST,), jnp.int32)
        .at[slot_of]
        .set(jnp.arange(row_count, dtype=jnp.int32))
    )
    filled = jnp.zeros((EXPERTS * MOST,), jnp.int32).at[slot_of].set(1)
    return (slot_of, token_of, filled)


def allowed_pairs(group_row, mask_row):
    row_count = group_row.shape[0]
    same_group = group_row[:, None] == group_row[None, :]
    diagonal = jnp.arange(row_count)[:, None] == jnp.arange(row_count)[None, :]
    return same_group & ((mask_row[None, :] == 1) | diagonal)


def head_slice(matrix, head_index):
    return lax.dynamic_slice_in_dim(matrix, head_index * HEAD_DIM, HEAD_DIM, 1)


def join_heads(stacked):
    return jnp.transpose(stacked, (1, 0, 2)).reshape(stacked.shape[1], HEADS * HEAD_DIM)


def attend_forward(query_rows, key_rows, value_rows, allowed):

    def one_head(head_index):
        query_head = head_slice(query_rows, head_index)
        key_head = head_slice(key_rows, head_index)
        value_head = head_slice(value_rows, head_index)
        scores = contract_cols(query_head, key_head) * score_scale
        scores = jnp.where(allowed, scores, -1e30)
        highest = jnp.max(scores, 1, keepdims=True)
        powers = jnp.exp(scores - highest)
        totals = jnp.sum(powers, 1, keepdims=True)
        probs = (powers / totals).astype(jnp.bfloat16)
        context = jnp.dot(probs, value_head, preferred_element_type=jnp.float32)
        return (context, (highest + jnp.log(totals))[:, 0])

    contexts, log_totals = lax.map(one_head, jnp.arange(HEADS, dtype=jnp.int32))
    return (join_heads(contexts), log_totals)


def attend_backward(query_rows, key_rows, value_rows, allowed, log_totals, context_grad):

    def one_head(head_index):
        query_head = head_slice(query_rows, head_index)
        key_head = head_slice(key_rows, head_index)
        value_head = head_slice(value_rows, head_index)
        grad_head = head_slice(context_grad, head_index)
        scores = contract_cols(query_head, key_head) * score_scale
        probs = jnp.where(allowed, jnp.exp(scores - log_totals[head_index][:, None]), 0.0)
        prob_grad = contract_cols(grad_head, value_head)
        inner = jnp.sum(probs * prob_grad, 1, keepdims=True)
        score_grad = (probs * (prob_grad - inner)).astype(jnp.bfloat16)
        query_grad = score_scale * jnp.dot(score_grad, key_head, preferred_element_type=jnp.float32)
        key_grad = score_scale * contract_rows(score_grad, query_head)
        value_grad = contract_rows(probs.astype(jnp.bfloat16), grad_head)
        return (query_grad, key_grad, value_grad)

    parts = lax.map(one_head, jnp.arange(HEADS, dtype=jnp.int32))
    return tuple((join_heads(part).astype(jnp.bfloat16) for part in parts))


def layer_forward(inputs, allowed, tables, attention, experts_full):
    query_weight, key_weight, value_weight, output_weight, first_gain, second_gain = attention
    weight_in, weight_out = experts_full
    width = inputs.shape[1]
    normed = layer_norm(inputs, first_gain.astype(jnp.float32)).astype(jnp.bfloat16)
    query_rows = jnp.dot(normed, query_weight, preferred_element_type=jnp.float32).astype(
        jnp.bfloat16
    )
    key_rows = jnp.dot(normed, key_weight, preferred_element_type=jnp.float32).astype(jnp.bfloat16)
    value_rows = jnp.dot(normed, value_weight, preferred_element_type=jnp.float32).astype(
        jnp.bfloat16
    )
    context, log_totals = attend_forward(query_rows, key_rows, value_rows, allowed)
    context = context.astype(jnp.bfloat16)
    hidden_in = inputs + jnp.dot(context, output_weight, preferred_element_type=jnp.float32)
    second = layer_norm(hidden_in, second_gain.astype(jnp.float32)).astype(jnp.bfloat16)
    slot_of, token_of, filled = tables
    slot_rows = jnp.where(filled[:, None] == 1, second[token_of], jnp.zeros((), jnp.bfloat16))
    everyone = lax.all_gather(slot_rows, "expert", axis=0, tiled=True)
    grouped = everyone.reshape(-1, EXPERTS, MOST, width)
    before = jnp.einsum("demc,ecf->demf", grouped, weight_in, preferred_element_type=jnp.float32)
    activated = jax.nn.gelu(before, approximate=False).astype(jnp.bfloat16)
    partial_sums = jnp.einsum(
        "demf,efc->demc", activated, weight_out, preferred_element_type=jnp.float32
    )
    own_sums = lax.psum_scatter(
        partial_sums.reshape(-1, width).astype(jnp.bfloat16),
        "expert",
        scatter_dimension=0,
        tiled=True,
    ).astype(jnp.float32)
    outputs = hidden_in + own_sums[slot_of]
    kept = (
        inputs,
        normed,
        query_rows,
        key_rows,
        value_rows,
        log_totals,
        context,
        hidden_in,
        grouped,
        before,
        activated,
    )
    return (outputs, kept)


def layer_backward(grad_outputs, allowed, tables, attention, experts_full, kept):
    query_weight, key_weight, value_weight, output_weight, first_gain, second_gain = attention
    weight_in, weight_out = experts_full
    (
        inputs,
        normed,
        query_rows,
        key_rows,
        value_rows,
        log_totals,
        context,
        hidden_in,
        grouped,
        before,
        activated,
    ) = kept
    slot_of, token_of, filled = tables
    width = grad_outputs.shape[1]
    hidden_units = weight_in.shape[2]
    out_grad = grad_outputs.astype(jnp.bfloat16)
    slot_grads = jnp.where(filled[:, None] == 1, out_grad[token_of], jnp.zeros((), jnp.bfloat16))
    every_grad = lax.all_gather(slot_grads, "expert", axis=0, tiled=True).reshape(grouped.shape)
    active_grad = jnp.einsum(
        "demc,efc->demf", every_grad, weight_out, preferred_element_type=jnp.float32
    )
    _, slope_back = jax.vjp(partial(jax.nn.gelu, approximate=False), before)
    before_grad = slope_back(active_grad)[0].astype(jnp.bfloat16)
    expert_rows = weight_in.shape[1] // lax.axis_size("dp")
    in_term = jnp.einsum("demc,demf->cef", grouped, before_grad, preferred_element_type=jnp.float32)
    out_term = jnp.einsum(
        "demf,demc->cef", activated, every_grad, preferred_element_type=jnp.float32
    )
    expert_total = lax.psum_scatter(
        jnp.stack([in_term, out_term], 1).reshape(
            lax.axis_size("dp") * expert_rows, 2 * EXPERTS * hidden_units
        ),
        "dp",
        scatter_dimension=0,
        tiled=True,
    )
    expert_total = expert_total.reshape(expert_rows, 2, EXPERTS, hidden_units)
    in_weight_grad = jnp.transpose(expert_total[:, 0], (1, 0, 2))
    out_weight_grad = jnp.transpose(expert_total[:, 1], (1, 2, 0))
    input_part = jnp.einsum(
        "demf,ecf->demc", before_grad, weight_in, preferred_element_type=jnp.float32
    )
    slot_input = lax.psum_scatter(
        input_part.reshape(-1, width).astype(jnp.bfloat16),
        "expert",
        scatter_dimension=0,
        tiled=True,
    ).astype(jnp.float32)
    second_grad = slot_input[slot_of]
    _, second_back = jax.vjp(layer_norm, hidden_in, second_gain.astype(jnp.float32))
    hidden_norm_grad, second_gain_grad = second_back(second_grad)
    hidden_grad = grad_outputs + hidden_norm_grad
    branch_grad = hidden_grad.astype(jnp.bfloat16)
    context_grad = contract_cols(branch_grad, output_weight).astype(jnp.bfloat16)
    query_grad, key_grad, value_grad = attend_backward(
        query_rows, key_rows, value_rows, allowed, log_totals, context_grad
    )
    normed_grad = (
        contract_cols(query_grad, query_weight)
        + contract_cols(key_grad, key_weight)
        + contract_cols(value_grad, value_weight)
    )
    attention_total = lax.psum_scatter(
        jnp.concatenate(
            [
                contract_rows(normed, query_grad),
                contract_rows(normed, key_grad),
                contract_rows(normed, value_grad),
                contract_rows(context, branch_grad),
            ],
            1,
        ),
        ("dp", "expert"),
        scatter_dimension=0,
        tiled=True,
    )
    _, first_back = jax.vjp(layer_norm, inputs, first_gain.astype(jnp.float32))
    input_norm_grad, first_gain_grad = first_back(normed_grad)
    input_grad = hidden_grad + input_norm_grad
    gain_total = (
        lax.psum_scatter(first_gain_grad, ("dp", "expert"), scatter_dimension=0, tiled=True),
        lax.psum_scatter(second_gain_grad, ("dp", "expert"), scatter_dimension=0, tiled=True),
    )
    attention_part = (
        attention_total[:, 0:width],
        attention_total[:, width : 2 * width],
        attention_total[:, 2 * width : 3 * width],
        attention_total[:, 3 * width : 4 * width],
        gain_total[0],
        gain_total[1],
    )
    return (input_grad, attention_part, (in_weight_grad, out_weight_grad))


def on_device(
    tokens,
    groups,
    key_mask,
    routes,
    query_weight,
    key_weight,
    value_weight,
    output_weight,
    norm_first,
    norm_second,
    expert_in,
    expert_out,
    cotangent,
):
    allowed = allowed_pairs(groups[0], key_mask)
    tables = slot_tables(routes[:, 0])
    state = tokens.astype(jnp.float32)
    saved = []
    for layer_index in range(LAYERS):
        attention = (
            lax.all_gather(query_weight[layer_index], ("dp", "expert"), axis=0, tiled=True),
            lax.all_gather(key_weight[layer_index], ("dp", "expert"), axis=0, tiled=True),
            lax.all_gather(value_weight[layer_index], ("dp", "expert"), axis=0, tiled=True),
            lax.all_gather(output_weight[layer_index], ("dp", "expert"), axis=0, tiled=True),
            lax.all_gather(norm_first[layer_index], ("dp", "expert"), axis=0, tiled=True),
            lax.all_gather(norm_second[layer_index], ("dp", "expert"), axis=0, tiled=True),
        )
        experts_full = (
            lax.all_gather(expert_in[layer_index], "dp", axis=1, tiled=True),
            lax.all_gather(expert_out[layer_index], "dp", axis=2, tiled=True),
        )
        state, kept = layer_forward(state, allowed, tables, attention, experts_full)
        saved.append((attention, experts_full, kept))
    mixed = state.astype(jnp.bfloat16)
    grad_state = cotangent
    results = [None] * LAYERS
    for layer_index in reversed(range(LAYERS)):
        attention, experts_full, kept = saved[layer_index]
        attention = (
            lax.all_gather(query_weight[layer_index], ("dp", "expert"), axis=0, tiled=True),
            lax.all_gather(key_weight[layer_index], ("dp", "expert"), axis=0, tiled=True),
            lax.all_gather(value_weight[layer_index], ("dp", "expert"), axis=0, tiled=True),
            lax.all_gather(output_weight[layer_index], ("dp", "expert"), axis=0, tiled=True),
            lax.all_gather(norm_first[layer_index], ("dp", "expert"), axis=0, tiled=True),
            lax.all_gather(norm_second[layer_index], ("dp", "expert"), axis=0, tiled=True),
        )
        experts_full = (
            lax.all_gather(expert_in[layer_index], "dp", axis=1, tiled=True),
            lax.all_gather(expert_out[layer_index], "dp", axis=2, tiled=True),
        )
        grad_state, attention_part, expert_part = layer_backward(
            grad_state, allowed, tables, attention, experts_full, kept
        )
        results[layer_index] = (attention_part, expert_part)
    delta_query = jnp.stack([results[index][0][0] for index in range(LAYERS)])
    delta_key = jnp.stack([results[index][0][1] for index in range(LAYERS)])
    delta_value = jnp.stack([results[index][0][2] for index in range(LAYERS)])
    delta_output = jnp.stack([results[index][0][3] for index in range(LAYERS)])
    delta_first = jnp.stack([results[index][0][4] for index in range(LAYERS)])
    delta_second = jnp.stack([results[index][0][5] for index in range(LAYERS)])
    delta_in = jnp.stack([results[index][1][0] for index in range(LAYERS)])
    delta_out = jnp.stack([results[index][1][1] for index in range(LAYERS)])
    return (
        mixed,
        grad_state,
        delta_query,
        delta_key,
        delta_value,
        delta_output,
        delta_first,
        delta_second,
        delta_in,
        delta_out,
    )


def solution(mesh):
    placed = (
        P(("dp", "expert"), None),
        P(("dp", "expert"), None),
        P(("dp", "expert")),
        P(("dp", "expert"), None),
        P(None, ("dp", "expert"), None),
        P(None, ("dp", "expert"), None),
        P(None, ("dp", "expert"), None),
        P(None, ("dp", "expert"), None),
        P(None, ("dp", "expert")),
        P(None, ("dp", "expert")),
        P(None, None, "dp", "expert"),
        P(None, None, "expert", "dp"),
        P(("dp", "expert"), None),
    )
    return jax.shard_map(
        on_device,
        mesh=mesh,
        in_specs=placed,
        out_specs=(
            P(("dp", "expert"), None),
            P(("dp", "expert"), None),
            P(None, ("dp", "expert"), None),
            P(None, ("dp", "expert"), None),
            P(None, ("dp", "expert"), None),
            P(None, ("dp", "expert"), None),
            P(None, ("dp", "expert")),
            P(None, ("dp", "expert")),
            P(None, None, "dp", "expert"),
            P(None, None, "expert", "dp"),
        ),
        check_vma=False,
    )
```

profile of v0, /device:TPU:0, one launch (start us, length us, event | category | flops | bytes accessed | tf_op | source)
XLA Modules:
  0.0 1962.7 jit_solution(9064034768107004105)
XLA Ops:
  16.4 42.1 %all-reduce.9 = (bf16[768]{0:T(1024)(128)(2,1)S(1)}, bf16[768]{0:T(1024)(128)(2,1)S(1)}, bf16[768]{0:T(1024)(128)(2,1)}, bf16[768]{0:T(1024)(128)(2,1)}) all-reduce(bf16[768]{0:T(1024)(128)(2,1)S(1)} %dynamic-update-slice, bf16[768]{0:T(1024)(128)(2,1)S(1)} %dynamic-update-slice.1, ...), channel_id=2, replica_groups=mesh['dp'=8,'expert'=4] {'dp','expert'}, use_global_device_ids=true, to_apply=%add | all-reduce | flops 3072 | bytes 12288
  70.7 54.2 %all-gather.43.cloned.1.call-done = bf16[1,768,768]{2,1,0:T(8,128)(2,1)} async-done(((bf16[1,24,768]{2,1,0:T(8,128)(2,1)}), bf16[1,768,768]{2,1,0:T(8,128)(2,1)}) %all-gather.43.cloned.1.call-update) | async-done | bytes 1179664 | tf_op jit(solution)/shard_map/all_gather | solution.py:275
  126.9 54.5 %all-gather.41.cloned.1.call-done = bf16[1,768,768]{2,1,0:T(8,128)(2,1)} async-done(((bf16[1,24,768]{2,1,0:T(8,128)(2,1)}), bf16[1,768,768]{2,1,0:T(8,128)(2,1)}) %all-gather.41.cloned.1.call-update) | async-done | bytes 1179664 | tf_op jit(solution)/shard_map/all_gather | solution.py:274
  184.6 57.9 %while.56 = (s32[]{:T(128)}, bf16[12,384,64]{1,2,0:T(8,128)(2,1)S(1)}, f32[12,384]{1,0:T(8,128)}, s32[12]{0:T(128)}, bf16[384,768]{1,0:T(8,128)(2,1)S(1)}, /*ind...) while((s32[]{:T(128)}, ...), condition=%wide.region_5.6_spmd.clone, body=%wide.region_2.0_spmd.clone.sunk | while | flops 39517828 | bytes 2187971 | solution.py:82
  251.2 53.3 %all-gather.49.cloned.1.call-done = bf16[1,3,768,768]{3,2,1,0:T(8,128)(2,1)} async-done(((bf16[1,3,96,768]{3,2,1,0:T(8,128)(2,1)}), bf16[1,3,768,768]{3,2,1,0:T(8,128)(2,1)}) %all-gather.49.cloned.1.call-update) | async-done | bytes 3538960 | tf_op jit(solution)/shard_map/all_gather | solution.py:282
  304.6 26.2 %all-gather.33.cloned.1.call-done = bf16[1728,768]{1,0:T(8,128)(2,1)} async-done(((bf16[432,768]{1,0:T(8,128)(2,1)}), bf16[1728,768]{1,0:T(8,128)(2,1)}) %all-gather.33.cloned.1.call-update) | async-done | bytes 2654224 | tf_op jit(solution)/shard_map/all_gather | solution.py:125
  330.8 16.5 fusion.101
  347.3 51.5 %all-gather.51.cloned.1.call-done = bf16[1,3,768,768]{2,3,1,0:T(8,128)(2,1)} async-done(((bf16[1,3,768,96]{2,3,1,0:T(8,128)(2,1)}), bf16[1,3,768,768]{2,3,1,0:T(8,128)(2,1)}) %all-gather.51.cloned.1.call-update) | async-done | bytes 3538960 | tf_op jit(solution)/shard_map/all_gather | solution.py:283
  411.8 27.2 %reduce-scatter.13.cloned.1.call-done = bf16[432,768]{1,0:T(8,128)(2,1)} async-done(((bf16[1728,768]{1,0:T(8,128)(2,1)}), bf16[432,768]{1,0:T(8,128)(2,1)}) %reduce-scatter.13.cloned.1.call-update) | async-done | bytes 663568 | tf_op jit(solution)/shard_map/reduce_scatter | solution.py:132
  444.7 51.7 %all-gather.57.cloned.1.call-done = bf16[1,768,768]{2,1,0:T(8,128)(2,1)} async-done(((bf16[1,24,768]{2,1,0:T(8,128)(2,1)}), bf16[1,768,768]{2,1,0:T(8,128)(2,1)}) %all-gather.57.cloned.1.call-update) | async-done | bytes 1179664 | tf_op jit(solution)/shard_map/all_gather | solution.py:276
  499.2 54.0 %all-gather.55.cloned.1.call-done = bf16[1,768,768]{2,1,0:T(8,128)(2,1)} async-done(((bf16[1,24,768]{2,1,0:T(8,128)(2,1)}), bf16[1,768,768]{2,1,0:T(8,128)(2,1)}) %all-gather.55.cloned.1.call-update) | async-done | bytes 1179664 | tf_op jit(solution)/shard_map/all_gather | solution.py:275
  555.9 54.1 %all-gather.53.cloned.1.call-done = bf16[1,768,768]{2,1,0:T(8,128)(2,1)} async-done(((bf16[1,24,768]{2,1,0:T(8,128)(2,1)}), bf16[1,768,768]{2,1,0:T(8,128)(2,1)}) %all-gather.53.cloned.1.call-update) | async-done | bytes 1179664 | tf_op jit(solution)/shard_map/all_gather | solution.py:274
  614.8 78.2 %while.57 = (s32[]{:T(128)}, bf16[12,384,64]{1,2,0:T(8,128)(2,1)}, f32[12,384]{1,0:T(8,128)}, s32[12]{0:T(128)}, bf16[384,768]{1,0:T(8,128)(2,1)}, /*index=5*/bf...) while((s32[]{:T(128)}, bf16[12,384,64]{1,2,0:T(8,128)(2,1)}, ...), condition=%wide.region_19.20_spmd.clone, body=%wide.region_16.19_spmd.clone.sunk | while | flops 39517828 | bytes 2187455 | solution.py:82
  702.9 30.5 %all-gather.61.cloned.1.call-done = bf16[1,3,768,768]{3,2,1,0:T(8,128)(2,1)} async-done(((bf16[1,3,96,768]{3,2,1,0:T(8,128)(2,1)}), bf16[1,3,768,768]{3,2,1,0:T(8,128)(2,1)}) %all-gather.61.cloned.1.call-update) | async-done | bytes 3538960 | tf_op jit(solution)/shard_map/all_gather | solution.py:282
  733.4 26.3 %all-gather.35.cloned.1.call-done = bf16[1728,768]{1,0:T(8,128)(2,1)} async-done(((bf16[432,768]{1,0:T(8,128)(2,1)}), bf16[1728,768]{1,0:T(8,128)(2,1)}) %all-gather.35.cloned.1.call-update) | async-done | bytes 2654224 | tf_op jit(solution)/shard_map/all_gather | solution.py:125
  759.7 16.5 fusion.99
  776.3 51.0 %all-gather.63.cloned.1.call-done = bf16[1,3,768,768]{2,3,1,0:T(8,128)(2,1)} async-done(((bf16[1,3,768,96]{2,3,1,0:T(8,128)(2,1)}), bf16[1,3,768,768]{2,3,1,0:T(8,128)(2,1)}) %all-gather.63.cloned.1.call-update) | async-done | bytes 3538960 | tf_op jit(solution)/shard_map/all_gather | solution.py:283
  827.2 26.3 %all-gather.37.cloned.1.call-done = bf16[1728,768]{1,0:T(8,128)(2,1)} async-done(((bf16[432,768]{1,0:T(8,128)(2,1)}), bf16[1728,768]{1,0:T(8,128)(2,1)}) %all-gather.37.cloned.1.call-update) | async-done | bytes 2654224 | tf_op jit(solution)/shard_map/all_gather | solution.py:176
  874.2 27.8 %reduce-scatter.17.cloned.1.call-done = bf16[432,768]{1,0:T(8,128)(2,1)} async-done(((bf16[1728,768]{1,0:T(8,128)(2,1)}), bf16[432,768]{1,0:T(8,128)(2,1)}) %reduce-scatter.17.cloned.1.call-update) | async-done | bytes 663568 | tf_op jit(solution)/shard_map/reduce_scatter | solution.py:201
  908.3 31.0 %reduce-scatter.15.cloned.1.call-done = bf16[432,768]{1,0:T(8,128)(2,1)} async-done(((bf16[1728,768]{1,0:T(8,128)(2,1)}), bf16[432,768]{1,0:T(8,128)(2,1)}) %reduce-scatter.15.cloned.1.call-update) | async-done | bytes 663568 | tf_op jit(solution)/shard_map/reduce_scatter | solution.py:132
  951.8 146.1 %while.58 = (s32[]{:T(128)}, bf16[12,384,64]{1,2,0:T(8,128)(2,1)}, bf16[12,384,64]{1,2,0:T(8,128)(2,1)}, bf16[12,384,64]{1,2,0:T(8,128)(2,1)}, s32[12]{0:T(128)S...) while((s32[]{:T(128)}, bf16[12,384,64]{1,2,0:T(8,128)(2,1)}, ...), condition=%wide.region_28.29_spmd.clone, body=%wide.region_26.28_spmd.clone.sunk | while | flops 96337536 | bytes 5422857 | solution.py:103
  1111.3 25.7 %all-gather.39.cloned.1.call-done = bf16[1728,768]{1,0:T(8,128)(2,1)} async-done(((bf16[432,768]{1,0:T(8,128)(2,1)}), bf16[1728,768]{1,0:T(8,128)(2,1)}) %all-gather.39.cloned.1.call-update) | async-done | bytes 2654224 | tf_op jit(solution)/shard_map/all_gather | solution.py:176
  1160.0 9.8 copy.89
  1170.1 15.2 reduce-scatter.19.cloned.1.call-done
  1196.9 132.3 %while.59 = (s32[]{:T(128)}, bf16[12,384,64]{1,2,0:T(8,128)(2,1)S(1)}, bf16[12,384,64]{1,2,0:T(8,128)(2,1)}, bf16[12,384,64]{1,2,0:T(8,128)(2,1)S(1)}, s32[12]{0...) while((s32[]{:T(128)}, ...), condition=%wide.region_36.37_spmd.clone, body=%wide.region_34.36_spmd.clone.sunk | while | flops 96337536 | bytes 5422857 | solution.py:103
  1360.8 12.8 pad_maximum_fusion.1
  1373.7 15.6 copy.76
  1403.4 11.8 pad_maximum_fusion
  1415.2 15.4 copy.73
  1435.8 40.5 %all-reduce.8 = (f32[768]{0:T(1024)S(1)}, f32[768]{0:T(1024)S(1)}, f32[768]{0:T(1024)S(1)}, f32[768]{0:T(1024)S(1)}) all-reduce(f32[768]{0:T(1024)} %get-tuple-element.358, f32[768]{0:T(1024)S(1)} %get-tuple-element.360, f32[768]{0:T(1024)S(1)} %copy-done.62, ...), channel_id=25, replica_groups=mesh['dp'=8,'expert'=4] {'dp','expert'}, use_global_device_ids=true, to_apply=%region_44.45.clone | all-reduce | flops 3072 | bytes 24576
  1486.8 228.4 %reduce-scatter.23.cloned.1.call-done = f32[96,4608]{1,0:T(8,128)} async-done(((f32[768,4608]{1,0:T(8,128)}), f32[96,4608]{1,0:T(8,128)}) %reduce-scatter.23.cloned.1.call-update) | async-done | bytes 1769488 | tf_op jit(solution)/shard_map/reduce_scatter | solution.py:187
  1719.6 227.4 %reduce-scatter.21.cloned.1.call-done = f32[96,4608]{1,0:T(8,128)} async-done(((f32[768,4608]{1,0:T(8,128)}), f32[96,4608]{1,0:T(8,128)}) %reduce-scatter.21.cloned.1.call-update) | async-done | bytes 1769488 | tf_op jit(solution)/shard_map/reduce_scatter | solution.py:187
  (755 shorter events, 569.7 us)
Async XLA Ops:
  7.2 61.5 %all-gather.45.cloned.1.call-start = ((), (), s32[]{:S(2)}) async-start(), calls=%async_computation.20 | async-start | bytes 1216512 | tf_op jit(solution)/shard_map/all_gather | solution.py:276
  8.8 116.2 %all-gather.43.cloned.1.call-start = ((), (), s32[]{:S(2)}) async-start(), calls=%async_computation.19 | async-start | bytes 1216512 | tf_op jit(solution)/shard_map/all_gather | solution.py:275
  10.3 171.1 %all-gather.41.cloned.1.call-start = ((), (), s32[]{:S(2)}) async-start(), calls=%async_computation.18 | async-start | bytes 1216512 | tf_op jit(solution)/shard_map/all_gather | solution.py:274
  11.8 230.8 %all-gather.47.cloned.1.call-start = ((), (), s32[]{:S(2)}) async-start(), calls=%async_computation.21 | async-start | bytes 1216512 | tf_op jit(solution)/shard_map/all_gather | solution.py:277
  13.3 291.3 %all-gather.49.cloned.1.call-start = ((), (), s32[]{:S(2)}) async-start(), calls=%async_computation.22 | async-start | bytes 3981312 | tf_op jit(solution)/shard_map/all_gather | solution.py:282
  15.5 315.3 %all-gather.33.cloned.1.call-start = ((), (), s32[]{:S(2)}) async-start(), calls=%async_computation.8 | async-start | bytes 3317760 | tf_op jit(solution)/shard_map/all_gather | solution.py:125
  58.6 122.9 %copy-start.34 = (f32[768]{0:T(1024)}, f32[768]{0:T(1024)S(1)}, u32[]{:S(2)}) copy-start(f32[768]{0:T(1024)S(1)} %convert_element_type.296) | copy-start | bytes 9220
  60.3 185.9 %copy-start.40 = (f32[768]{0:T(1024)}, f32[768]{0:T(1024)S(1)}, u32[]{:S(2)}) copy-start(f32[768]{0:T(1024)S(1)} %convert_element_type.297) | copy-start | bytes 9220
  249.6 149.2 %all-gather.51.cloned.1.call-start = ((), (), s32[]{:S(2)}) async-start(), calls=%async_computation.23 | async-start | bytes 3981312 | tf_op jit(solution)/shard_map/all_gather | solution.py:283
  251.0 188.1 %reduce-scatter.13.cloned.1.call-start = ((), (), s32[]{:S(2)}) async-start(), calls=%async_computation.9 | async-start | bytes 3317760 | tf_op jit(solution)/shard_map/reduce_scatter | solution.py:132
  405.6 90.9 %all-gather.57.cloned.1.call-start = ((), (), s32[]{:S(2)}) async-start(), calls=%async_computation.26 | async-start | bytes 1216512 | tf_op jit(solution)/shard_map/all_gather | solution.py:276
  406.3 146.9 %all-gather.55.cloned.1.call-start = ((), (), s32[]{:S(2)}) async-start(), calls=%async_computation.25 | async-start | bytes 1216512 | tf_op jit(solution)/shard_map/all_gather | solution.py:275
  406.9 203.2 %all-gather.53.cloned.1.call-start = ((), (), s32[]{:S(2)}) async-start(), calls=%async_computation.24 | async-start | bytes 1216512 | tf_op jit(solution)/shard_map/all_gather | solution.py:274
  407.6 285.3 %all-gather.59.cloned.1.call-start = ((), (), s32[]{:S(2)}) async-start(), calls=%async_computation.27 | async-start | bytes 1216512 | tf_op jit(solution)/shard_map/all_gather | solution.py:277
  408.2 325.2 %all-gather.61.cloned.1.call-start = ((), (), s32[]{:S(2)}) async-start(), calls=%async_computation.28 | async-start | bytes 3981312 | tf_op jit(solution)/shard_map/all_gather | solution.py:282
  408.9 350.8 %all-gather.35.cloned.1.call-start = ((), (), s32[]{:S(2)}) async-start(), calls=%async_computation.10 | async-start | bytes 3317760 | tf_op jit(solution)/shard_map/all_gather | solution.py:125
  444.2 248.8 %copy-start.2 = (f32[384,768]{1,0:T(8,128)}, f32[384,768]{1,0:T(8,128)S(1)}, u32[]{:S(2)}) copy-start(f32[384,768]{1,0:T(8,128)S(1)} %get-tuple-element.463) | copy-start | bytes 3538948
  701.5 125.7 %all-gather.63.cloned.1.call-start = ((), (), s32[]{:S(2)}) async-start(), calls=%async_computation.29 | async-start | bytes 3981312 | tf_op jit(solution)/shard_map/all_gather | solution.py:283
  702.1 151.5 %all-gather.37.cloned.1.call-start = ((), (), s32[]{:S(2)}) async-start(), calls=%async_computation.12 | async-start | bytes 3317760 | tf_op jit(solution)/shard_map/all_gather | solution.py:176
  702.7 199.3 %reduce-scatter.17.cloned.1.call-start = ((), (), s32[]{:S(2)}) async-start(), calls=%async_computation.13 | async-start | bytes 3317760 | tf_op jit(solution)/shard_map/reduce_scatter | solution.py:201
  866.9 72.4 %reduce-scatter.15.cloned.1.call-start = ((), (), s32[]{:S(2)}) async-start(), calls=%async_computation.11 | async-start | bytes 3317760 | tf_op jit(solution)/shard_map/reduce_scatter | solution.py:132
  873.7 263.3 %all-gather.39.cloned.1.call-start = ((), (), s32[]{:S(2)}) async-start(), calls=%async_computation.14 | async-start | bytes 3317760 | tf_op jit(solution)/shard_map/all_gather | solution.py:176
  947.6 207.5 %copy-start.4 = (f32[384,768]{1,0:T(8,128)}, f32[384,768]{1,0:T(8,128)S(1)}, u32[]{:S(2)}) copy-start(f32[384,768]{1,0:T(8,128)S(1)} %add_add_fusion.7) | copy-start | bytes 3538948
  1111.1 74.3 %reduce-scatter.19.cloned.1.call-start = ((), (), s32[]{:S(2)}) async-start(), calls=%async_computation.15 | async-start | bytes 3317760 | tf_op jit(solution)/shard_map/reduce_scatter | solution.py:201
  1150.3 328.8 %reduce-scatter.27.cloned.1.call-start = ((), (), s32[]{:S(2)}) async-start(), calls=%async_computation.31 | async-start | bytes 9732096
  1169.8 313.2 %reduce-scatter.25.cloned.1.call-start = ((), (), s32[]{:S(2)}) async-start(), calls=%async_computation.30 | async-start | bytes 9732096
  1196.9 132.4 %copy-start.1 = (bf16[384,768]{1,0:T(8,128)(2,1)S(1)}, bf16[384,768]{1,0:T(8,128)(2,1)}, u32[]{:S(2)}) copy-start(bf16[384,768]{1,0:T(8,128)(2,1)} %param.21) | copy-start | bytes 1769476
  1196.9 132.4 %copy-start.35 = (f32[768]{0:T(1024)S(1)}, f32[768]{0:T(1024)}, u32[]{:S(2)}) copy-start(f32[768]{0:T(1024)} %copy-done.34) | copy-start | bytes 9220
  1196.9 132.4 %copy-start.37 = (f32[384]{0:T(512)S(1)}, f32[384]{0:T(512)}, u32[]{:S(2)}) copy-start(f32[384]{0:T(512)} %copy-done.36) | copy-start | bytes 4612
  1196.9 132.4 %copy-start.39 = (f32[384]{0:T(512)S(1)}, f32[384]{0:T(512)}, u32[]{:S(2)}) copy-start(f32[384]{0:T(512)} %copy-done.38) | copy-start | bytes 4612
  1346.9 368.3 %reduce-scatter.23.cloned.1.call-start = ((), (), s32[]{:S(2)}) async-start(), calls=%async_computation.17 | async-start | bytes 15925248 | tf_op jit(solution)/shard_map/reduce_scatter | solution.py:187
  1389.3 557.8 %reduce-scatter.21.cloned.1.call-start = ((), (), s32[]{:S(2)}) async-start(), calls=%async_computation.16 | async-start | bytes 15925248 | tf_op jit(solution)/shard_map/reduce_scatter | solution.py:187
  (75 other events, 1069.9 us)
Sparse Core Ops, SparseCore 0:
  11.5 56.7 all-gather.44
  71.8 53.1 all-gather.42
  128.4 52.9 all-gather.40
  184.7 53.0 all-gather.46
  240.4 64.1 all-gather.48
  306.6 24.2 all-gather.32
  333.6 65.1 all-gather.50
  405.7 33.3 reduce-scatter.12
  442.4 54.0 all-gather.56
  500.2 52.9 all-gather.54
  557.1 52.9 all-gather.52
  613.2 53.0 all-gather.58
  669.3 64.0 all-gather.60
  735.5 24.2 all-gather.34
  762.0 65.1 all-gather.62
  829.3 24.2 all-gather.36
  867.0 34.8 reduce-scatter.16
  904.4 34.8 reduce-scatter.14
  1111.2 25.7 all-gather.38
  1150.4 34.8 reduce-scatter.18
  1191.2 135.6 reduce-scatter.26
  1347.0 135.9 reduce-scatter.24
  1486.7 228.4 reduce-scatter.22
  1718.7 228.2 reduce-scatter.20
where the time goes:
time: 1980 us; the launch traced here: 1960 us
  waiting for transfers between devices  1120 us (57%)
  matrix products  369 us (19%)
  local copies, waits for them, and re-layouts  220 us (11%)
  blocking collectives  82.7 us (4%)
  loops' own time  79.3 us (4%)
  other arithmetic  70.6 us (4%)
    reduce_scatter x2, waiting for transfers between devices, layer_backward(): lax.psum_scatter(jnp.stack([in_term, out_term], 1).reshape(lax.axis_size(...  456 us
    all_gather x2, waiting for transfers between devices, on_device(): lax.all_gather(query_weight[layer_index], ('dp', 'expert'), axis=0, tiled...  109 us
    all_gather x2, waiting for transfers between devices, on_device(): lax.all_gather(key_weight[layer_index], ('dp', 'expert'), axis=0, tiled=T...  108 us
    dot_general x80, matrix products, contract_cols(): lax.dot_general(left, right, (((1,), (1,)), ((), ())), preferred_element_...  106 us
    all_gather x2, waiting for transfers between devices, on_device(): lax.all_gather(expert_out[layer_index], 'dp', axis=2, tiled=True)  102 us
    dot_general x56, matrix products, contract_rows(): lax.dot_general(left, right, (((0,), (0,)), ((), ())), preferred_element_...  89.6 us
    all_gather x2, waiting for transfers between devices, on_device(): lax.all_gather(expert_in[layer_index], 'dp', axis=1, tiled=True)  83.8 us
    unnamed x2, blocking collectives  82.7 us
  transfers between devices with their start and end apart: 24, of which 20 were waited for; matrix products, arithmetic and copies ran while one was open for 24% of the time, Pallas kernels for 0%

commit v1 on v0

--- a/solution.py
+++ b/solution.py
@@ -122,7 +122,14 @@
     second = layer_norm(hidden_in, second_gain.astype(jnp.float32)).astype(jnp.bfloat16)
     slot_of, token_of, filled = tables
     slot_rows = jnp.where(filled[:, None] == 1, second[token_of], jnp.zeros((), jnp.bfloat16))
-    everyone = lax.all_gather(slot_rows, "expert", axis=0, tiled=True)
+    ring = [slot_rows]
+    for hop in range(3):
+        ring.append(lax.ppermute(ring[-1], "expert", [(dev, (dev + 1) % 4) for dev in range(4)]))
+    everyone = jnp.roll(
+        jnp.concatenate(ring[::-1], axis=0),
+        (lax.axis_index("expert") + 1) * ring[0].shape[0],
+        axis=0,
+    )
     grouped = everyone.reshape(-1, EXPERTS, MOST, width)
     before = jnp.einsum("demc,ecf->demf", grouped, weight_in, preferred_element_type=jnp.float32)
     activated = jax.nn.gelu(before, approximate=False).astype(jnp.bfloat16)

time: 1980 us -> 1920 us (0.970)
  waiting for transfers between devices: 1120 us -> 1020 us
  other arithmetic: 70.6 us -> 106 us
    all_gather x2, waiting for transfers between devices: 83.8 us -> 5.79 us  [on_device(): lax.all_gather(expert_in[layer_index], 'dp', axis=1, tiled=True)]
    ppermute x0 -> x6, waiting for transfers between devices: none -> 57.9 us  [layer_forward(): lax.ppermute(ring[-1], 'expert', [(dev, (dev + 1) % 4) for dev in range(4)])]
    all_gather x2 -> x0, waiting for transfers between devices: 52.6 us -> none  [layer_forward(): everyone = lax.all_gather(slot_rows, 'expert', axis=0, tiled=True)]
    concatenate x0 -> x2, other arithmetic: none -> 36.1 us  [layer_forward(): jnp.roll(jnp.concatenate(ring[::-1], axis=0), (lax.axis_index('expert') +...]
  transfers between devices with their start and end apart: 24 -> 28, of which waited for: 20 -> 23; matrix products, arithmetic and copies ran while one was open for 24% -> 27% of each run, Pallas kernels for 0% -> 0%
where the time goes in v1:
time: 1920 us; the launch traced here: 1900 us
  waiting for transfers between devices  1020 us (53%)
  matrix products  369 us (19%)
  local copies, waits for them, and re-layouts  220 us (11%)
  other arithmetic  106 us (6%)
  blocking collectives  82.8 us (4%)
  loops' own time  79.4 us (4%)
    reduce_scatter x2, waiting for transfers between devices, layer_backward(): lax.psum_scatter(jnp.stack([in_term, out_term], 1).reshape(lax.axis_size(...  456 us
    all_gather x2, waiting for transfers between devices, on_device(): lax.all_gather(query_weight[layer_index], ('dp', 'expert'), axis=0, tiled...  109 us
    all_gather x2, waiting for transfers between devices, on_device(): lax.all_gather(key_weight[layer_index], ('dp', 'expert'), axis=0, tiled=T...  108 us
    dot_general x80, matrix products, contract_cols(): lax.dot_general(left, right, (((1,), (1,)), ((), ())), preferred_element_...  106 us
    dot_general x56, matrix products, contract_rows(): lax.dot_general(left, right, (((0,), (0,)), ((), ())), preferred_element_...  89.5 us
    all_gather x2, waiting for transfers between devices, on_device(): lax.all_gather(expert_out[layer_index], 'dp', axis=2, tiled=True)  83.1 us
    unnamed x2, blocking collectives  82.8 us
    another operation x2, loops' own time, attend_backward(): parts = lax.map(one_head, jnp.arange(HEADS, dtype=jnp.int32))  63.2 us
  transfers between devices with their start and end apart: 28, of which 23 were waited for; matrix products, arithmetic and copies ran while one was open for 27% of the time, Pallas kernels for 0%

profile of v1, /device:TPU:0, one launch (start us, length us, event | category | flops | bytes accessed | tf_op | source)
XLA Modules:
  0.0 1899.0 jit_solution(1908586595621498170)
XLA Ops:
  16.4 42.2 %all-reduce.9 = (bf16[768]{0:T(1024)(128)(2,1)S(1)}, bf16[768]{0:T(1024)(128)(2,1)S(1)}, bf16[768]{0:T(1024)(128)(2,1)}, bf16[768]{0:T(1024)(128)(2,1)}) all-reduce(bf16[768]{0:T(1024)(128)(2,1)S(1)} %dynamic-update-slice, bf16[768]{0:T(1024)(128)(2,1)S(1)} %dynamic-update-slice.1, ...), channel_id=2, replica_groups=mesh['dp'=8,'expert'=4] {'dp','expert'}, use_global_device_ids=true, to_apply=%add | all-reduce | flops 3072 | bytes 12288
  70.7 54.2 %all-gather.37.cloned.1.call-done = bf16[1,768,768]{2,1,0:T(8,128)(2,1)} async-done(((bf16[1,24,768]{2,1,0:T(8,128)(2,1)}), bf16[1,768,768]{2,1,0:T(8,128)(2,1)}) %all-gather.37.cloned.1.call-update) | async-done | bytes 1179664 | tf_op jit(solution)/shard_map/all_gather | solution.py:282
  126.9 54.5 %all-gather.35.cloned.1.call-done = bf16[1,768,768]{2,1,0:T(8,128)(2,1)} async-done(((bf16[1,24,768]{2,1,0:T(8,128)(2,1)}), bf16[1,768,768]{2,1,0:T(8,128)(2,1)}) %all-gather.35.cloned.1.call-update) | async-done | bytes 1179664 | tf_op jit(solution)/shard_map/all_gather | solution.py:281
  184.6 57.7 %while.56 = (s32[]{:T(128)}, bf16[12,384,64]{1,2,0:T(8,128)(2,1)S(1)}, f32[12,384]{1,0:T(8,128)}, s32[12]{0:T(128)}, bf16[384,768]{1,0:T(8,128)(2,1)S(1)}, /*ind...) while((s32[]{:T(128)}, ...), condition=%wide.region_5.6_spmd.clone, body=%wide.region_2.0_spmd.clone.sunk | while | flops 39517828 | bytes 2187971 | solution.py:82
  258.7 10.1 collective-permute-done.1
  269.0 10.2 collective-permute-done.2
  279.2 19.6 %fusion.152 = bf16[1728,768]{1,0:T(8,128)(2,1)} fusion(s32[]{:T(128)S(6)} %select_n.98, bf16[432,768]{1,0:T(8,128)(2,1)} %collective-permute-done.2, bf16[432,768]{1,0:T(8,128)(2,1)S(1)} %collective-permute-done.1, bf16[432,768]{1,0:T(8,128)(2,1)S(1)} %collective-permute-done, bf16[432,768]{1,0:T(8,128)(2,1)S(1)} %broadcast_select_fusion.3), kind=kLoop, calls=%fused_computation.228 | loop fusion | flops 21233664 | bytes 5308420 | tf_op jit(solution)/shard_map/jit(_roll_dynamic)/concatenate | solution.py:128
  304.6 16.9 fusion.101
  321.5 49.4 %all-gather.45.cloned.1.call-done = bf16[1,3,768,768]{2,3,1,0:T(8,128)(2,1)} async-done(((bf16[1,3,768,96]{2,3,1,0:T(8,128)(2,1)}), bf16[1,3,768,768]{2,3,1,0:T(8,128)(2,1)}) %all-gather.45.cloned.1.call-update) | async-done | bytes 3538960 | tf_op jit(solution)/shard_map/all_gather | solution.py:290
  384.9 26.5 %reduce-scatter.13.cloned.1.call-done = bf16[432,768]{1,0:T(8,128)(2,1)} async-done(((bf16[1728,768]{1,0:T(8,128)(2,1)}), bf16[432,768]{1,0:T(8,128)(2,1)}) %reduce-scatter.13.cloned.1.call-update) | async-done | bytes 663568 | tf_op jit(solution)/shard_map/reduce_scatter | solution.py:139
  417.0 51.7 %all-gather.51.cloned.1.call-done = bf16[1,768,768]{2,1,0:T(8,128)(2,1)} async-done(((bf16[1,24,768]{2,1,0:T(8,128)(2,1)}), bf16[1,768,768]{2,1,0:T(8,128)(2,1)}) %all-gather.51.cloned.1.call-update) | async-done | bytes 1179664 | tf_op jit(solution)/shard_map/all_gather | solution.py:283
  471.4 54.2 %all-gather.49.cloned.1.call-done = bf16[1,768,768]{2,1,0:T(8,128)(2,1)} async-done(((bf16[1,24,768]{2,1,0:T(8,128)(2,1)}), bf16[1,768,768]{2,1,0:T(8,128)(2,1)}) %all-gather.49.cloned.1.call-update) | async-done | bytes 1179664 | tf_op jit(solution)/shard_map/all_gather | solution.py:282
  528.3 54.0 %all-gather.47.cloned.1.call-done = bf16[1,768,768]{2,1,0:T(8,128)(2,1)} async-done(((bf16[1,24,768]{2,1,0:T(8,128)(2,1)}), bf16[1,768,768]{2,1,0:T(8,128)(2,1)}) %all-gather.47.cloned.1.call-update) | async-done | bytes 1179664 | tf_op jit(solution)/shard_map/all_gather | solution.py:281
  587.1 78.2 %while.57 = (s32[]{:T(128)}, bf16[12,384,64]{1,2,0:T(8,128)(2,1)}, f32[12,384]{1,0:T(8,128)}, s32[12]{0:T(128)}, bf16[384,768]{1,0:T(8,128)(2,1)}, /*index=5*/bf...) while((s32[]{:T(128)}, bf16[12,384,64]{1,2,0:T(8,128)(2,1)}, ...), condition=%wide.region_19.21_spmd.clone, body=%wide.region_16.20_spmd.clone.sunk | while | flops 39517828 | bytes 2187455 | solution.py:82
  694.8 10.1 collective-permute-done.5
  704.9 16.5 fusion.145
  721.4 16.7 fusion.99
  738.2 33.7 %all-gather.57.cloned.1.call-done = bf16[1,3,768,768]{2,3,1,0:T(8,128)(2,1)} async-done(((bf16[1,3,768,96]{2,3,1,0:T(8,128)(2,1)}), bf16[1,3,768,768]{2,3,1,0:T(8,128)(2,1)}) %all-gather.57.cloned.1.call-update) | async-done | bytes 3538960 | tf_op jit(solution)/shard_map/all_gather | solution.py:290
  778.7 19.5 %all-gather.31.cloned.1.call-done = bf16[1728,768]{1,0:T(8,128)(2,1)} async-done(((bf16[432,768]{1,0:T(8,128)(2,1)}), bf16[1728,768]{1,0:T(8,128)(2,1)}) %all-gather.31.cloned.1.call-update) | async-done | bytes 2654224 | tf_op jit(solution)/shard_map/all_gather | solution.py:183
  811.4 24.2 %reduce-scatter.15.cloned.1.call-done = bf16[432,768]{1,0:T(8,128)(2,1)} async-done(((bf16[1728,768]{1,0:T(8,128)(2,1)}), bf16[432,768]{1,0:T(8,128)(2,1)}) %reduce-scatter.15.cloned.1.call-update) | async-done | bytes 663568 | tf_op jit(solution)/shard_map/reduce_scatter | solution.py:139
  839.5 33.4 %reduce-scatter.17.cloned.1.call-done = bf16[432,768]{1,0:T(8,128)(2,1)} async-done(((bf16[1728,768]{1,0:T(8,128)(2,1)}), bf16[432,768]{1,0:T(8,128)(2,1)}) %reduce-scatter.17.cloned.1.call-update) | async-done | bytes 663568 | tf_op jit(solution)/shard_map/reduce_scatter | solution.py:208
  887.5 146.0 %while.58 = (s32[]{:T(128)}, bf16[12,384,64]{1,2,0:T(8,128)(2,1)}, bf16[12,384,64]{1,2,0:T(8,128)(2,1)}, bf16[12,384,64]{1,2,0:T(8,128)(2,1)}, s32[12]{0:T(128)S...) while((s32[]{:T(128)}, bf16[12,384,64]{1,2,0:T(8,128)(2,1)}, ...), condition=%wide.region_28.30_spmd.clone, body=%wide.region_26.29_spmd.clone.sunk | while | flops 96337536 | bytes 5422857 | solution.py:103
  1047.3 25.4 %all-gather.33.cloned.1.call-done = bf16[1728,768]{1,0:T(8,128)(2,1)} async-done(((bf16[432,768]{1,0:T(8,128)(2,1)}), bf16[1728,768]{1,0:T(8,128)(2,1)}) %all-gather.33.cloned.1.call-update) | async-done | bytes 2654224 | tf_op jit(solution)/shard_map/all_gather | solution.py:183
  1105.8 15.3 reduce-scatter.19.cloned.1.call-done
  1132.8 132.3 %while.59 = (s32[]{:T(128)}, bf16[12,384,64]{1,2,0:T(8,128)(2,1)S(1)}, bf16[12,384,64]{1,2,0:T(8,128)(2,1)}, bf16[12,384,64]{1,2,0:T(8,128)(2,1)S(1)}, s32[12]{0...) while((s32[]{:T(128)}, ...), condition=%wide.region_36.38_spmd.clone, body=%wide.region_34.37_spmd.clone.sunk | while | flops 96337536 | bytes 5422857 | solution.py:103
  1296.7 12.8 pad_maximum_fusion.1
  1309.5 15.6 copy.76
  1339.0 11.9 pad_maximum_fusion
  1350.9 15.3 copy.73
  1371.4 40.7 %all-reduce.8 = (f32[768]{0:T(1024)S(1)}, f32[768]{0:T(1024)S(1)}, f32[768]{0:T(1024)S(1)}, f32[768]{0:T(1024)S(1)}) all-reduce(f32[768]{0:T(1024)} %get-tuple-element.359, f32[768]{0:T(1024)S(1)} %get-tuple-element.361, f32[768]{0:T(1024)S(1)} %copy-done.65, ...), channel_id=25, replica_groups=mesh['dp'=8,'expert'=4] {'dp','expert'}, use_global_device_ids=true, to_apply=%region_44.46.clone | all-reduce | flops 3072 | bytes 24576
  1423.0 228.1 %reduce-scatter.23.cloned.1.call-done = f32[96,4608]{1,0:T(8,128)} async-done(((f32[768,4608]{1,0:T(8,128)}), f32[96,4608]{1,0:T(8,128)}) %reduce-scatter.23.cloned.1.call-update) | async-done | bytes 1769488 | tf_op jit(solution)/shard_map/reduce_scatter | solution.py:194
  1655.5 227.5 %reduce-scatter.21.cloned.1.call-done = f32[96,4608]{1,0:T(8,128)} async-done(((f32[768,4608]{1,0:T(8,128)}), f32[96,4608]{1,0:T(8,128)}) %reduce-scatter.21.cloned.1.call-update) | async-done | bytes 1769488 | tf_op jit(solution)/shard_map/reduce_scatter | solution.py:194
  (765 shorter events, 613.3 us)
Async XLA Ops:
  7.2 61.5 %all-gather.39.cloned.1.call-start = ((), (), s32[]{:S(2)}) async-start(), calls=%async_computation.18 | async-start | bytes 1216512 | tf_op jit(solution)/shard_map/all_gather | solution.py:283
  8.8 116.2 %all-gather.37.cloned.1.call-start = ((), (), s32[]{:S(2)}) async-start(), calls=%async_computation.17 | async-start | bytes 1216512 | tf_op jit(solution)/shard_map/all_gather | solution.py:282
  10.3 171.1 %all-gather.35.cloned.1.call-start = ((), (), s32[]{:S(2)}) async-start(), calls=%async_computation.16 | async-start | bytes 1216512 | tf_op jit(solution)/shard_map/all_gather | solution.py:281
  11.8 230.6 %all-gather.41.cloned.1.call-start = ((), (), s32[]{:S(2)}) async-start(), calls=%async_computation.19 | async-start | bytes 1216512 | tf_op jit(solution)/shard_map/all_gather | solution.py:284
  13.3 291.3 %all-gather.43.cloned.1.call-start = ((), (), s32[]{:S(2)}) async-start(), calls=%async_computation.20 | async-start | bytes 3981312 | tf_op jit(solution)/shard_map/all_gather | solution.py:289
  15.5 355.5 %all-gather.45.cloned.1.call-start = ((), (), s32[]{:S(2)}) async-start(), calls=%async_computation.21 | async-start | bytes 3981312 | tf_op jit(solution)/shard_map/all_gather | solution.py:290
  60.3 185.7 %copy-start.43 = (f32[768]{0:T(1024)}, f32[768]{0:T(1024)S(1)}, u32[]{:S(2)}) copy-start(f32[768]{0:T(1024)S(1)} %convert_element_type.297) | copy-start | bytes 9220
  248.6 10.1 collective-permute-start
  251.0 160.3 %reduce-scatter.13.cloned.1.call-start = ((), (), s32[]{:S(2)}) async-start(), calls=%async_computation.8 | async-start | bytes 3317760 | tf_op jit(solution)/shard_map/reduce_scatter | solution.py:139
  258.7 10.1 collective-permute-start.1
  268.8 10.4 collective-permute-start.2
  377.8 90.9 %all-gather.51.cloned.1.call-start = ((), (), s32[]{:S(2)}) async-start(), calls=%async_computation.24 | async-start | bytes 1216512 | tf_op jit(solution)/shard_map/all_gather | solution.py:283
  378.6 147.0 %all-gather.49.cloned.1.call-start = ((), (), s32[]{:S(2)}) async-start(), calls=%async_computation.23 | async-start | bytes 1216512 | tf_op jit(solution)/shard_map/all_gather | solution.py:282
  379.3 203.0 %all-gather.47.cloned.1.call-start = ((), (), s32[]{:S(2)}) async-start(), calls=%async_computation.22 | async-start | bytes 1216512 | tf_op jit(solution)/shard_map/all_gather | solution.py:281
  379.9 285.3 %all-gather.53.cloned.1.call-start = ((), (), s32[]{:S(2)}) async-start(), calls=%async_computation.25 | async-start | bytes 1216512 | tf_op jit(solution)/shard_map/all_gather | solution.py:284
  380.6 340.8 %all-gather.55.cloned.1.call-start = ((), (), s32[]{:S(2)}) async-start(), calls=%async_computation.26 | async-start | bytes 3981312 | tf_op jit(solution)/shard_map/all_gather | solution.py:289
  381.2 390.6 %all-gather.57.cloned.1.call-start = ((), (), s32[]{:S(2)}) async-start(), calls=%async_computation.27 | async-start | bytes 3981312 | tf_op jit(solution)/shard_map/all_gather | solution.py:290
  382.0 416.2 %all-gather.31.cloned.1.call-start = ((), (), s32[]{:S(2)}) async-start(), calls=%async_computation.10 | async-start | bytes 3317760 | tf_op jit(solution)/shard_map/all_gather | solution.py:183
  416.5 248.8 %copy-start.2 = (f32[384,768]{1,0:T(8,128)}, f32[384,768]{1,0:T(8,128)S(1)}, u32[]{:S(2)}) copy-start(f32[384,768]{1,0:T(8,128)S(1)} %get-tuple-element.464) | copy-start | bytes 3538948
  674.4 10.1 collective-permute-start.3
  684.5 10.3 collective-permute-start.4
  694.7 10.2 collective-permute-start.5
  694.8 140.8 %reduce-scatter.15.cloned.1.call-start = ((), (), s32[]{:S(2)}) async-start(), calls=%async_computation.9 | async-start | bytes 3317760 | tf_op jit(solution)/shard_map/reduce_scatter | solution.py:139
  778.6 94.3 %reduce-scatter.17.cloned.1.call-start = ((), (), s32[]{:S(2)}) async-start(), calls=%async_computation.11 | async-start | bytes 3317760 | tf_op jit(solution)/shard_map/reduce_scatter | solution.py:208
  811.4 261.3 %all-gather.33.cloned.1.call-start = ((), (), s32[]{:S(2)}) async-start(), calls=%async_computation.12 | async-start | bytes 3317760 | tf_op jit(solution)/shard_map/all_gather | solution.py:183
  883.4 207.4 %copy-start.4 = (f32[384,768]{1,0:T(8,128)}, f32[384,768]{1,0:T(8,128)S(1)}, u32[]{:S(2)}) copy-start(f32[384,768]{1,0:T(8,128)S(1)} %add_add_fusion.7) | copy-start | bytes 3538948
  1046.8 74.2 %reduce-scatter.19.cloned.1.call-start = ((), (), s32[]{:S(2)}) async-start(), calls=%async_computation.13 | async-start | bytes 3317760 | tf_op jit(solution)/shard_map/reduce_scatter | solution.py:208
  1086.0 328.8 %reduce-scatter.27.cloned.1.call-start = ((), (), s32[]{:S(2)}) async-start(), calls=%async_computation.29 | async-start | bytes 9732096
  1105.5 313.7 %reduce-scatter.25.cloned.1.call-start = ((), (), s32[]{:S(2)}) async-start(), calls=%async_computation.28 | async-start | bytes 9732096
  1132.7 132.4 %copy-start.1 = (bf16[384,768]{1,0:T(8,128)(2,1)S(1)}, bf16[384,768]{1,0:T(8,128)(2,1)}, u32[]{:S(2)}) copy-start(bf16[384,768]{1,0:T(8,128)(2,1)} %param.23) | copy-start | bytes 1769476
  1282.8 368.3 %reduce-scatter.23.cloned.1.call-start = ((), (), s32[]{:S(2)}) async-start(), calls=%async_computation.15 | async-start | bytes 15925248 | tf_op jit(solution)/shard_map/reduce_scatter | solution.py:194
  1325.1 557.9 %reduce-scatter.21.cloned.1.call-start = ((), (), s32[]{:S(2)}) async-start(), calls=%async_computation.14 | async-start | bytes 15925248 | tf_op jit(solution)/shard_map/reduce_scatter | solution.py:194
  (80 other events, 1604.1 us)
Sparse Core Ops, SparseCore 0:
  11.5 56.7 all-gather.38
  71.8 53.0 all-gather.36
  128.4 52.9 all-gather.34
  184.8 53.0 all-gather.40
  240.5 64.0 all-gather.42
  307.2 63.6 all-gather.44
  378.0 33.3 reduce-scatter.12
  414.6 54.0 all-gather.50
  472.6 52.9 all-gather.48
  529.3 52.9 all-gather.46
  585.6 52.9 all-gather.52
  641.5 64.0 all-gather.54
  708.1 63.6 all-gather.56
  773.9 24.2 all-gather.30
  800.7 34.8 reduce-scatter.14
  838.0 34.8 reduce-scatter.16
  1046.9 25.7 all-gather.32
  1086.1 34.8 reduce-scatter.18
  1126.9 135.5 reduce-scatter.26
  1282.9 136.2 reduce-scatter.24
  1422.9 228.1 reduce-scatter.22
  1654.7 228.2 reduce-scatter.20
